TPU v7x, 32 devices: a whole 2x2x4 slice. The times are simulated.
32 devices in a mesh: blk: 4 (over x, core), grp: 8 (over z, y).
Axes of the slice: x: 2, y: 2, z: 4, core: 2. Of those that a mesh axis runs over, the one named last changes fastest.
Arguments:
- picture_vectors: bfloat16 [12288, 1152], P(('blk', 'grp')), may hold values from -2.3570226 to 2.3570226
- text_vectors: bfloat16 [12288, 1152], P(('blk', 'grp')), may hold values from -2.3570226 to 2.3570226
- matching_text_position: int32 [32, 384], P(('blk', 'grp')), may hold values from 0 to 383, each once within a row
- natural_scale_exponent: float32 [1], replicated, may hold values from 1.5 to 2.3
- offset_added_before_sigmoid: float32 [1], replicated, may hold values from -3 to -1
Outputs:
- image_grad: bfloat16 [12288, 1152], P(('blk', 'grp'))
- caption_grad: bfloat16 [12288, 1152], P(('blk', 'grp'))
Inputs may be any that keep to these rules, and one draw needn't show every extreme that they name: `matching_text_position`: each row of positives names every position 0 .. 383 exactly once.
All inputs are finite; a program needn't handle non-finite values.
Results may differ from a plain program's by a relative error of at most 0.0059.
Values may be sent and summed in bfloat16 or wider, within the bound.
A program may use at most 64 MiB of HBM per device.

v0:
```python
import functools

import jax
import jax.numpy as jnp
from jax import lax
from jax.experimental import pallas as pl
from jax.experimental.pallas import tpu as pltpu
from jax.sharding import PartitionSpec as P

CHUNKS = 3
NORM_ROWS = 32
MESH = pl.DeviceIdType.MESH

A0, A1, A2, A3, B0, B1, B2, B3 = range(8)
(
    OWN_A_PAIR,
    OWN_A_FAR,
    A1_FAR,
    A2_PAIR,
    OWN_B_FAR,
    B2_PAIR,
    SUM_B1,
    SUM_B3,
    SUM_A3,
    SUM_A1,
    SUM_A2,
    SUM_B2,
) = range(12)


def kernel(
    groups,
    total,
    image_hbm,
    text_hbm,
    position_hbm,
    exponent_ref,
    offset_ref,
    image_out,
    text_out,
    image_ref,
    text_ref,
    position_ref,
    image_unit,
    captions,
    coefs,
    partial,
    staged,
    returned,
    direction,
    image_inverse,
    text_inverse,
    load_sem,
    send_sem,
    recv_sem,
):
    rows, width = image_hbm.shape
    half = rows // 2
    chunk = half // CHUNKS
    me = lax.axis_index("blk") * groups + lax.axis_index("grp")
    parity = lax.rem(me, 2)
    step = 1 - 2 * parity

    def place(index):
        index = lax.rem(index + total, total)
        return (index // groups, lax.rem(index, groups))

    pair = place(me + step)
    ahead = place(me + 2 * step)
    behind = place(me - 2 * step)

    barrier = pltpu.get_barrier_semaphore()
    for device in (pair, ahead, behind):
        pl.semaphore_signal(barrier, inc=1, device_id=device, device_id_type=MESH)

    start_a = pl.multiple_of(parity * half, half)
    start_b = pl.multiple_of(half - parity * half, half)

    def load(n, source, target):
        return pltpu.make_async_copy(source, target, load_sem.at[n])

    half_a, half_b = (pl.ds(start_a, half), pl.ds(start_b, half))
    loads = (
        load(0, text_hbm.at[half_b], text_ref.at[half_b]),
        load(1, text_hbm.at[half_a], text_ref.at[half_a]),
        load(2, image_hbm, image_ref),
        load(3, position_hbm, position_ref),
    )
    for copy in loads:
        copy.start()

    def piece(c):
        return pl.ds(c * chunk, chunk)

    def message(name, c, source, target, device):
        return pltpu.make_async_remote_copy(
            src_ref=source.at[piece(c)],
            dst_ref=target.at[piece(c)],
            send_sem=send_sem.at[name, c],
            recv_sem=recv_sem.at[name, c],
            device_id=device,
            device_id_type=MESH,
        )

    routes = {
        OWN_A_PAIR: (captions.at[A0], captions.at[B1], pair),
        OWN_A_FAR: (captions.at[A0], captions.at[A2], ahead),
        A1_FAR: (captions.at[A1], captions.at[A3], ahead),
        A2_PAIR: (captions.at[A2], captions.at[B3], pair),
        OWN_B_FAR: (captions.at[B0], captions.at[B2], behind),
        B2_PAIR: (captions.at[B2], captions.at[A1], pair),
        SUM_B1: (staged.at[0], returned.at[0], pair),
        SUM_B3: (staged.at[1], returned.at[1], pair),
        SUM_A3: (staged.at[2], returned.at[2], behind),
        SUM_A1: (staged.at[3], returned.at[3], pair),
        SUM_A2: (staged.at[4], returned.at[4], behind),
        SUM_B2: (staged.at[5], returned.at[5], ahead),
    }

    def send(name, c):
        message(name, c, *routes[name]).start()

    def receive(name, c):
        message(name, c, *routes[name]).wait_recv()

    def normalize(source, inverse, slot_ref, source_start):
        def body(i, carry):
            at = pl.multiple_of(i * NORM_ROWS, NORM_ROWS)
            here = pl.ds(pl.multiple_of(source_start + at, NORM_ROWS), NORM_ROWS)
            values = source[here, :].astype(jnp.float32)
            scale = lax.rsqrt(jnp.sum(values * values, axis=1, keepdims=True) + 1e-06)
            inverse[here, :] = scale
            slot_ref[pl.ds(at, NORM_ROWS), :] = (values * scale).astype(jnp.bfloat16)
            return carry

        lax.fori_loop(0, slot_ref.shape[0] // NORM_ROWS, body, 0)

    loads[0].wait()
    normalize(text_ref, text_inverse, captions.at[B0], start_b)
    pl.semaphore_wait(barrier, 3)
    for c in range(CHUNKS):
        send(OWN_B_FAR, c)
    loads[1].wait()
    normalize(text_ref, text_inverse, captions.at[A0], start_a)
    send(OWN_A_PAIR, 0)
    send(OWN_A_FAR, 0)
    for load in loads[2:]:
        load.wait()
    normalize(image_ref, image_inverse, image_unit, 0)

    scale = jnp.exp(jnp.full((1, rows), exponent_ref[0], jnp.float32))
    offset = offset_ref[0]

    def tile(slot, c, first_row=None):
        text = captions[slot, piece(c), :]
        logit = (
            lax.dot_general(
                text,
                image_unit[...],
                (((1,), (1,)), ((), ())),
                preferred_element_type=jnp.float32,
            )
            * scale
            + offset
        )
        if first_row is None:
            coef = scale * jax.nn.sigmoid(logit)
        else:
            row = lax.broadcasted_iota(jnp.int32, logit.shape, 0) + first_row + c * chunk
            polarity = jnp.where(row == position_ref[0:1, :], 1.0, -1.0)
            coef = scale * (-polarity * jax.nn.sigmoid(-polarity * logit))
        coef = coef.astype(jnp.bfloat16)
        coefs[slot, piece(c), :] = coef
        return jnp.dot(coef, image_unit[...], preferred_element_type=jnp.float32)

    def relay(name, c, source, buffer, slot, part):
        receive(source, c)
        arrived = returned[buffer, piece(c), :].astype(jnp.float32)
        staged[slot, piece(c), :] = (arrived + partial[part, piece(c), :]).astype(
            jnp.bfloat16
        )
        send(name, c)

    tile_width = 384 if width % 384 == 0 else 128

    def accumulate(i, carry):
        lanes = pl.ds(pl.multiple_of(i * tile_width, 128), tile_width)
        result = jnp.zeros((rows, tile_width), jnp.float32)
        for slot in range(8):
            result += lax.dot_general(
                coefs[slot],
                captions[slot, :, lanes],
                (((0,), (0,)), ((), ())),
                preferred_element_type=jnp.float32,
            )
        direction[:, lanes] = result
        return carry

    def finish(source, inverse, here, value):
        scale = inverse[here, :]
        flat = source[here, :].astype(jnp.float32) * scale
        cosine = jnp.sum(flat * value, axis=1, keepdims=True)
        return (scale * (value - flat * cosine)).astype(jnp.bfloat16)

    def finish_images(i, carry):
        here = pl.ds(pl.multiple_of(i * NORM_ROWS, NORM_ROWS), NORM_ROWS)
        image_out[here, :] = finish(image_ref, image_inverse, here, direction[here, :])
        return carry


    def finish_text(c, start, part, buffers):
        def body(i, carry):
            at = pl.multiple_of(c * chunk + i * NORM_ROWS, NORM_ROWS)
            local = pl.ds(at, NORM_ROWS)
            here = pl.ds(pl.multiple_of(start + at, NORM_ROWS), NORM_ROWS)
            value = partial[part, local, :]
            for buffer in buffers:
                value += returned[buffer, local, :].astype(jnp.float32)
            text_out[here, :] = finish(text_ref, text_inverse, here, value)
            return carry

        lax.fori_loop(0, chunk // NORM_ROWS, body, 0)

    def forward(arrival, name, c):
        receive(arrival, c)
        send(name, c)

    def keep(slot, part, c, first_row=None):
        partial[part, piece(c), :] = tile(slot, c, first_row)

    def give(arrival, slot, stage, c):
        receive(arrival, c)
        staged[stage, piece(c), :] = tile(slot, c).astype(jnp.bfloat16)

    def images():
        lax.fori_loop(0, width // tile_width, accumulate, 0)
        lax.fori_loop(0, rows // NORM_ROWS, finish_images, 0)

    for c in range(CHUNKS):
        forward(OWN_B_FAR, B2_PAIR, c)
        if c + 1 < CHUNKS:
            send(OWN_A_FAR, c + 1)
            send(OWN_A_PAIR, c + 1)
    for c in range(CHUNKS):
        forward(B2_PAIR, A1_FAR, c)
        forward(OWN_A_FAR, A2_PAIR, c)
    give(OWN_A_PAIR, B1, 0, 0)
    send(SUM_B1, 0)
    for c in range(1, CHUNKS):
        give(OWN_A_PAIR, B1, 0, c)

    for c in range(CHUNKS):
        keep(A1, 0, c)
        give(A1_FAR, A3, 2, c)
        send(SUM_A3, c)
        give(A2_PAIR, B3, 1, c)
        send(SUM_B3, c)
    for c in range(CHUNKS):
        keep(A2, 1, c)
        keep(B2, 2, c)

    for c in range(CHUNKS):
        relay(SUM_A1, c, SUM_A3, 2, 3, 0)
        relay(SUM_A2, c, SUM_B3, 1, 4, 1)
    for c in range(1, CHUNKS):
        send(SUM_B1, c)

    for c in range(CHUNKS):
        keep(A0, 3, c, start_a)
        keep(B0, 4, c, start_b)

    for c in range(CHUNKS):
        relay(SUM_B2, c, SUM_A1, 3, 5, 2)

    images()

    for c in range(CHUNKS):
        receive(SUM_B1, c)
        receive(SUM_A2, c)
        finish_text(c, start_a, 3, (0, 4))
    for c in range(CHUNKS):
        receive(SUM_B2, c)
        finish_text(c, start_b, 4, (5,))

    for name in routes:
        for c in range(CHUNKS):
            message(name, c, *routes[name]).wait_send()


def solution(mesh):
    groups = mesh.shape["grp"]
    total = mesh.shape["blk"] * groups

    def local(images, texts, positions, exponent, offset):
        rows, width = images.shape
        half = rows // 2
        vmem = pl.BlockSpec(memory_space=pltpu.VMEM)
        hbm = pl.BlockSpec(memory_space=pl.ANY)
        smem = pl.BlockSpec(memory_space=pltpu.SMEM)
        return pl.pallas_call(
            functools.partial(kernel, groups, total),
            out_shape=(
                jax.ShapeDtypeStruct((rows, width), jnp.bfloat16),
                jax.ShapeDtypeStruct((rows, width), jnp.bfloat16),
            ),
            in_specs=[hbm, hbm, hbm, smem, smem],
            out_specs=(vmem, vmem),
            scratch_shapes=[
                pltpu.VMEM((rows, width), jnp.bfloat16),
                pltpu.VMEM((rows, width), jnp.bfloat16),
                pltpu.VMEM((1, rows), jnp.int32),
                pltpu.VMEM((rows, width), jnp.bfloat16),
                pltpu.VMEM((8, half, width), jnp.bfloat16),
                pltpu.VMEM((8, half, rows), jnp.bfloat16),
                pltpu.VMEM((5, half, width), jnp.float32),
                pltpu.VMEM((6, half, width), jnp.bfloat16),
                pltpu.VMEM((6, half, width), jnp.bfloat16),
                pltpu.VMEM((rows, width), jnp.float32),
                pltpu.VMEM((rows, 1), jnp.float32),
                pltpu.VMEM((rows, 1), jnp.float32),
                pltpu.SemaphoreType.DMA((4,)),
                pltpu.SemaphoreType.DMA((12, CHUNKS)),
                pltpu.SemaphoreType.DMA((12, CHUNKS)),
            ],
            compiler_params=pltpu.CompilerParams(
                collective_id=0, has_side_effects=True, vmem_limit_bytes=60 * 1024 * 1024
            ),
        )(images, texts, positions, exponent, offset)

    shard = P(("blk", "grp"), None)
    return jax.shard_map(
        local,
        mesh=mesh,
        in_specs=(shard, shard, shard, P(), P()),
        out_specs=(shard, shard),
        check_vma=False,
    )
```

profile of v0, /device:TPU:0, one launch (start us, length us, event | category | flops | bytes accessed | tf_op | source)
XLA Modules:
  0.0 75.9 jit_solution(14508615713471708579)
XLA Ops:
  1.9 70.8 %shard_map.68 = (bf16[384,1152]{1,0:T(8,128)(2,1)}, bf16[384,1152]{1,0:T(8,128)(2,1)}) custom-call(bf16[384,1152]{1,0:T(8,128)(2,1)} %image_hbm.1, bf16[384,1152]{1,0:T(8,128)(2,1)} %text_hbm.1, s32[1,384]{1,0:T(1,128)} %position_hbm.1, f32[1]{0:T(128)S(6)} %copy.9.exponent_ref, f32[1]{0:T(128)S(6)} %copy.10.offset_ref), custom_call_target="tpu_custom_call" | custom-call | tf_op jit(solution)/shard_map/pallas_call | solution.py:300
  72.7 0.0 copy-start
  72.8 2.2 %copy.11 = bf16[384,1152]{1,0:T(8,128)(2,1)} copy(bf16[384,1152]{1,0:T(8,128)(2,1)} %get-tuple-element.4) | data formatting | bytes 1769472
  75.0 0.0 copy-done
  75.0 0.9 %copy.12 = bf16[384,1152]{1,0:T(8,128)(2,1)} copy(bf16[384,1152]{1,0:T(8,128)(2,1)S(1)} %copy-done) | data formatting | bytes 1769472
Async XLA Ops:
  72.7 2.2 %copy-start = (bf16[384,1152]{1,0:T(8,128)(2,1)S(1)}, bf16[384,1152]{1,0:T(8,128)(2,1)}, u32[]{:S(2)}) copy-start(bf16[384,1152]{1,0:T(8,128)(2,1)} %get-tuple-element.5) | copy-start | bytes 2654212
where the time goes:
time: 76.1 us; the launch traced here: 75.9 us
  Pallas kernels  70.8 us (93%)
  local copies, waits for them, and re-layouts  3.14 us (4%)
  between operations  1.94 us (3%)
    pallas_call x1, Pallas kernels, local(): pl.pallas_call(functools.partial(kernel, groups, total), out_shape=(jax.S...  70.8 us
    unnamed x4, local copies, waits for them, and re-layouts  3.14 us

commit v1 on v0

--- a/solution.py
+++ b/solution.py
@@ -287,6 +287,17 @@
             message(name, c, *routes[name]).wait_send()
 
 
+def store(image_grad, text_grad, image_out, text_out, sem):
+    copies = (
+        pltpu.make_async_copy(image_grad, image_out, sem.at[0]),
+        pltpu.make_async_copy(text_grad, text_out, sem.at[1]),
+    )
+    for copy in copies:
+        copy.start()
+    for copy in copies:
+        copy.wait()
+
+
 def solution(mesh):
     groups = mesh.shape["grp"]
     total = mesh.shape["blk"] * groups
@@ -295,13 +306,16 @@
         rows, width = images.shape
         half = rows // 2
         vmem = pl.BlockSpec(memory_space=pltpu.VMEM)
-        hbm = pl.BlockSpec(memory_space=pl.ANY)
+        hbm = pl.BlockSpec(memory_space=pltpu.HBM)
         smem = pl.BlockSpec(memory_space=pltpu.SMEM)
-        return pl.pallas_call(
+        images, texts, positions = (
+            pltpu.with_memory_space_constraint(x, pltpu.HBM) for x in (images, texts, positions)
+        )
+        grads = pl.pallas_call(
             functools.partial(kernel, groups, total),
             out_shape=(
-                jax.ShapeDtypeStruct((rows, width), jnp.bfloat16),
-                jax.ShapeDtypeStruct((rows, width), jnp.bfloat16),
+                pltpu.VMEM((rows, width), jnp.bfloat16),
+                pltpu.VMEM((rows, width), jnp.bfloat16),
             ),
             in_specs=[hbm, hbm, hbm, smem, smem],
             out_specs=(vmem, vmem),
@@ -323,9 +337,17 @@
                 pltpu.SemaphoreType.DMA((12, CHUNKS)),
             ],
             compiler_params=pltpu.CompilerParams(
-                collective_id=0, has_side_effects=True, vmem_limit_bytes=60 * 1024 * 1024
+                collective_id=0, has_side_effects=True, vmem_limit_bytes=24 * 1024 * 1024
             ),
         )(images, texts, positions, exponent, offset)
+        grads = tuple(pltpu.with_memory_space_constraint(g, pltpu.VMEM) for g in grads)
+        return pl.pallas_call(
+            store,
+            out_shape=(jax.ShapeDtypeStruct((rows, width), jnp.bfloat16),) * 2,
+            in_specs=[vmem, vmem],
+            out_specs=(hbm, hbm),
+            scratch_shapes=[pltpu.SemaphoreType.DMA((2,))],
+        )(*grads)
 
     shard = P(("blk", "grp"), None)
     return jax.shard_map(

time: 76.1 us -> 72.9 us (0.958)
  local copies, waits for them, and re-layouts: 3.14 us -> 0 us
    unnamed x4 -> x0, local copies, waits for them, and re-layouts: 3.14 us -> none
    pallas_call x1 -> x2, Pallas kernels: 70.8 us -> 70.8 us  [the longest x1 69.6 us: local(): pl.pallas_call(functools.partial(kernel, groups, total), out_shape=(pltpu...]
where the time goes in v1:
time: 72.9 us; the launch traced here: 72.7 us
  Pallas kernels  70.8 us (97%)
  between operations  1.93 us (3%)
    pallas_call x1, Pallas kernels, local(): pl.pallas_call(functools.partial(kernel, groups, total), out_shape=(pltpu...  69.6 us

profile of v1, /device:TPU:0, one launch (start us, length us, event | category | flops | bytes accessed | tf_op | source)
XLA Modules:
  0.0 72.7 jit_solution(1133399483697822648)
XLA Ops:
  1.9 69.6 %shard_map.68 = (bf16[384,1152]{1,0:T(8,128)(2,1)S(1)}, bf16[384,1152]{1,0:T(8,128)(2,1)S(1)}) custom-call(bf16[384,1152]{1,0:T(8,128)(2,1)} %image_hbm.1, bf16[384,1152]{1,0:T(8,128)(2,1)} %text_hbm.1, s32[1,384]{1,0:T(1,128)} %position_hbm.1, f32[1]{0:T(128)S(6)} %copy.7.exponent_ref, f32[1]{0:T(128)S(6)} %copy.8.offset_ref), custom_call_target="tpu_custom_call" | custom-call | tf_op jit(solution)/shard_map/pallas_call | solution.py:314
  71.5 1.2 %shard_map.69 = (bf16[384,1152]{1,0:T(8,128)(2,1)}, bf16[384,1152]{1,0:T(8,128)(2,1)}) custom-call(bf16[384,1152]{1,0:T(8,128)(2,1)S(1)} %get-tuple-element.4.image_grad, bf16[384,1152]{1,0:T(8,128)(2,1)S(1)} %get-tuple-element.5.text_grad), custom_call_target="tpu_custom_call" | custom-call | tf_op jit(solution)/shard_map/pallas_call | solution.py:344

commit v2 on v1

v2 whole, which is shorter than its diff:
```python
import functools

import jax
import jax.numpy as jnp
from jax import lax
from jax.experimental import pallas as pl
from jax.experimental.pallas import tpu as pltpu
from jax.sharding import PartitionSpec as P

CHUNKS = 3
NORM_ROWS = 32
MESH = pl.DeviceIdType.MESH

F0, F1, F2, N0, N1 = range(5)
OWN_F0, OWN_F1, OWN_N0, OWN_N1, PAIR_F1, PAIR_F2, PAIR_N0, PAIR_N1 = range(8)
FAR, HOP, NEAR, SUM_F2, SUM_F1, SUM_N1, IMAGE, SUM_IMAGE = range(8)


def kernel(
    groups,
    total,
    image_hbm,
    text_hbm,
    position_hbm,
    exponent_ref,
    offset_ref,
    image_out,
    text_out,
    image_ref,
    text_ref,
    position_ref,
    image_unit,
    pair_unit,
    captions,
    coefs,
    partial,
    staged,
    returned,
    image_staged,
    image_returned,
    direction,
    image_inverse,
    text_inverse,
    load_sem,
    send_sem,
    recv_sem,
):
    rows, width = image_hbm.shape
    half = rows // 2
    chunk, band = half // CHUNKS, rows // CHUNKS
    me = lax.axis_index("blk") * groups + lax.axis_index("grp")
    parity = lax.rem(me, 2)
    reach = 4 * parity - 2

    def place(index):
        index = lax.rem(index + total, total)
        return (index // groups, lax.rem(index, groups))

    pair = place(me + 1 - 2 * parity)
    far = place(me + reach)
    near = place(me - reach)

    barrier = pltpu.get_barrier_semaphore()
    for device in (pair, far, near):
        pl.semaphore_signal(barrier, inc=1, device_id=device, device_id_type=MESH)

    start_f = pl.multiple_of(half - parity * half, half)
    start_n = pl.multiple_of(parity * half, half)

    def load(n, source, target):
        return pltpu.make_async_copy(source, target, load_sem.at[n])

    half_f, half_n = (pl.ds(start_f, half), pl.ds(start_n, half))
    loads = (
        load(0, text_hbm.at[half_f], text_ref.at[half_f]),
        load(1, text_hbm.at[half_n], text_ref.at[half_n]),
        load(2, image_hbm, image_ref),
        load(3, position_hbm, position_ref),
    )
    for copy in loads:
        copy.start()

    def piece(c):
        return pl.ds(c * chunk, chunk)

    def stripe(c):
        return pl.ds(c * band, band)

    routes = {
        FAR: (captions.at[F0], captions.at[F1], far, piece),
        HOP: (captions.at[F1], captions.at[F2], far, piece),
        NEAR: (captions.at[N0], captions.at[N1], near, piece),
        SUM_F2: (staged.at[0], returned.at[0], near, piece),
        SUM_F1: (staged.at[1], returned.at[1], near, piece),
        SUM_N1: (staged.at[2], returned.at[2], far, piece),
        IMAGE: (image_unit, pair_unit, pair, stripe),
        SUM_IMAGE: (image_staged, image_returned, pair, stripe),
    }

    def message(name, c):
        source, target, device, part = routes[name]
        return pltpu.make_async_remote_copy(
            src_ref=source.at[part(c)],
            dst_ref=target.at[part(c)],
            send_sem=send_sem.at[name, c],
            recv_sem=recv_sem.at[name, c],
            device_id=device,
            device_id_type=MESH,
        )

    def send(name, c):
        message(name, c).start()

    def receive(name, c):
        message(name, c).wait_recv()

    def normalize(source, inverse, target, source_start):
        def body(i, carry):
            at = pl.multiple_of(i * NORM_ROWS, NORM_ROWS)
            here = pl.ds(pl.multiple_of(source_start + at, NORM_ROWS), NORM_ROWS)
            values = source[here, :].astype(jnp.float32)
            scale = lax.rsqrt(jnp.sum(values * values, axis=1, keepdims=True) + 1e-06)
            inverse[here, :] = scale
            target[pl.ds(at, NORM_ROWS), :] = (values * scale).astype(jnp.bfloat16)
            return carry

        lax.fori_loop(0, target.shape[0] // NORM_ROWS, body, 0)

    loads[0].wait()
    normalize(text_ref, text_inverse, captions.at[F0], start_f)
    pl.semaphore_wait(barrier, 3)
    for c in range(CHUNKS):
        send(FAR, c)
    loads[1].wait()
    normalize(text_ref, text_inverse, captions.at[N0], start_n)
    for c in range(CHUNKS):
        send(NEAR, c)
    for copy in loads[2:]:
        copy.wait()
    normalize(image_ref, image_inverse, image_unit, 0)
    for c in range(CHUNKS):
        send(IMAGE, c)

    scale = jnp.exp(jnp.full((1, rows), exponent_ref[0], jnp.float32))
    offset = offset_ref[0]

    def tile(slot, images, table, c, first_row=None):
        text = captions[slot, piece(c), :]
        logit = (
            lax.dot_general(
                text,
                images[...],
                (((1,), (1,)), ((), ())),
                preferred_element_type=jnp.float32,
            )
            * scale
            + offset
        )
        if first_row is None:
            coef = scale * jax.nn.sigmoid(logit)
        else:
            row = lax.broadcasted_iota(jnp.int32, logit.shape, 0) + first_row + c * chunk
            polarity = jnp.where(row == position_ref[0:1, :], 1.0, -1.0)
            coef = scale * (-polarity * jax.nn.sigmoid(-polarity * logit))
        coef = coef.astype(jnp.bfloat16)
        coefs[table, piece(c), :] = coef
        return jnp.dot(coef, images[...], preferred_element_type=jnp.float32)

    def keep(part, c, value):
        partial[part, piece(c), :] = value

    def add(part, c, value):
        partial[part, piece(c), :] += value

    def give(stage, c, value):
        staged[stage, piece(c), :] = value.astype(jnp.bfloat16)

    def gather(c, terms):
        lanes = pl.ds(c * band, band)
        result = jnp.zeros((band, width), jnp.float32)
        for table, slot in terms:
            result += lax.dot_general(
                coefs[table, :, lanes],
                captions[slot],
                (((0,), (0,)), ((), ())),
                preferred_element_type=jnp.float32,
            )
        return result

    def finish(source, inverse, here, value):
        scale = inverse[here, :]
        flat = source[here, :].astype(jnp.float32) * scale
        cosine = jnp.sum(flat * value, axis=1, keepdims=True)
        return (scale * (value - flat * cosine)).astype(jnp.bfloat16)

    def finish_images(c):
        def body(i, carry):
            here = pl.ds(pl.multiple_of(c * band + i * NORM_ROWS, NORM_ROWS), NORM_ROWS)
            value = direction[here, :] + image_returned[here, :].astype(jnp.float32)
            image_out[here, :] = finish(image_ref, image_inverse, here, value)
            return carry

        lax.fori_loop(0, band // NORM_ROWS, body, 0)

    def finish_text(c, start, part, buffer):
        def body(i, carry):
            at = pl.multiple_of(c * chunk + i * NORM_ROWS, NORM_ROWS)
            local = pl.ds(at, NORM_ROWS)
            here = pl.ds(pl.multiple_of(start + at, NORM_ROWS), NORM_ROWS)
            value = partial[part, local, :] + returned[buffer, local, :].astype(jnp.float32)
            text_out[here, :] = finish(text_ref, text_inverse, here, value)
            return carry

        lax.fori_loop(0, chunk // NORM_ROWS, body, 0)

    for c in range(CHUNKS):
        keep(F0, c, tile(F0, image_unit, OWN_F0, c, start_f))
    for c in range(CHUNKS):
        receive(FAR, c)
        send(HOP, c)
        keep(N0, c, tile(N0, image_unit, OWN_N0, c, start_n))
    for c in range(CHUNKS):
        keep(F1, c, tile(F1, image_unit, OWN_F1, c))
    for c in range(CHUNKS):
        receive(NEAR, c)
        keep(N1, c, tile(N1, image_unit, OWN_N1, c))

    for c in range(CHUNKS):
        receive(IMAGE, c)
    for c in range(CHUNKS):
        give(2, c, partial[N1, piece(c), :] + tile(N1, pair_unit, PAIR_N1, c))
        send(SUM_N1, c)
    for c in range(CHUNKS):
        add(F1, c, tile(F1, pair_unit, PAIR_F1, c))
    for c in range(CHUNKS):
        receive(HOP, c)
        give(0, c, tile(F2, pair_unit, PAIR_F2, c))
        send(SUM_F2, c)
    for c in range(CHUNKS):
        add(N0, c, tile(N0, pair_unit, PAIR_N0, c))

    pair_terms = ((PAIR_F1, F1), (PAIR_F2, F2), (PAIR_N0, N0), (PAIR_N1, N1))
    for c in range(CHUNKS):
        image_staged[stripe(c), :] = gather(c, pair_terms).astype(jnp.bfloat16)
        send(SUM_IMAGE, c)

    for c in range(CHUNKS):
        receive(SUM_F2, c)
        arrived = returned[0, piece(c), :].astype(jnp.float32)
        give(1, c, arrived + partial[F1, piece(c), :])
        send(SUM_F1, c)

    own_terms = ((OWN_F0, F0), (OWN_F1, F1), (OWN_N0, N0), (OWN_N1, N1))
    for c in range(CHUNKS):
        direction[stripe(c), :] = gather(c, own_terms)
    for c in range(CHUNKS):
        receive(SUM_IMAGE, c)
        finish_images(c)
    for c in range(CHUNKS):
        receive(SUM_N1, c)
        finish_text(c, start_n, N0, 2)
    for c in range(CHUNKS):
        receive(SUM_F1, c)
        finish_text(c, start_f, F0, 1)

    for name in routes:
        for c in range(CHUNKS):
            message(name, c).wait_send()


def store(image_grad, text_grad, image_out, text_out, sem):
    copies = (
        pltpu.make_async_copy(image_grad, image_out, sem.at[0]),
        pltpu.make_async_copy(text_grad, text_out, sem.at[1]),
    )
    for copy in copies:
        copy.start()
    for copy in copies:
        copy.wait()


def solution(mesh):
    groups = mesh.shape["grp"]
    total = mesh.shape["blk"] * groups

    def local(images, texts, positions, exponent, offset):
        rows, width = images.shape
        half = rows // 2
        vmem = pl.BlockSpec(memory_space=pltpu.VMEM)
        hbm = pl.BlockSpec(memory_space=pltpu.HBM)
        smem = pl.BlockSpec(memory_space=pltpu.SMEM)
        images, texts, positions = (
            pltpu.with_memory_space_constraint(x, pltpu.HBM) for x in (images, texts, positions)
        )
        grads = pl.pallas_call(
            functools.partial(kernel, groups, total),
            out_shape=(
                pltpu.VMEM((rows, width), jnp.bfloat16),
                pltpu.VMEM((rows, width), jnp.bfloat16),
            ),
            in_specs=[hbm, hbm, hbm, smem, smem],
            out_specs=(vmem, vmem),
            scratch_shapes=[
                pltpu.VMEM((rows, width), jnp.bfloat16),
                pltpu.VMEM((rows, width), jnp.bfloat16),
                pltpu.VMEM((1, rows), jnp.int32),
                pltpu.VMEM((rows, width), jnp.bfloat16),
                pltpu.VMEM((rows, width), jnp.bfloat16),
                pltpu.VMEM((5, half, width), jnp.bfloat16),
                pltpu.VMEM((8, half, rows), jnp.bfloat16),
                pltpu.VMEM((5, half, width), jnp.float32),
                pltpu.VMEM((3, half, width), jnp.bfloat16),
                pltpu.VMEM((3, half, width), jnp.bfloat16),
                pltpu.VMEM((rows, width), jnp.bfloat16),
                pltpu.VMEM((rows, width), jnp.bfloat16),
                pltpu.VMEM((rows, width), jnp.float32),
                pltpu.VMEM((rows, 1), jnp.float32),
                pltpu.VMEM((rows, 1), jnp.float32),
                pltpu.SemaphoreType.DMA((4,)),
                pltpu.SemaphoreType.DMA((8, CHUNKS)),
                pltpu.SemaphoreType.DMA((8, CHUNKS)),
            ],
            compiler_params=pltpu.CompilerParams(
                collective_id=0, has_side_effects=True, vmem_limit_bytes=32 * 1024 * 1024
            ),
        )(images, texts, positions, exponent, offset)
        grads = tuple(pltpu.with_memory_space_constraint(g, pltpu.VMEM) for g in grads)
        return pl.pallas_call(
            store,
            out_shape=(jax.ShapeDtypeStruct((rows, width), jnp.bfloat16),) * 2,
            in_specs=[vmem, vmem],
            out_specs=(hbm, hbm),
            scratch_shapes=[pltpu.SemaphoreType.DMA((2,))],
        )(*grads)

    shard = P(("blk", "grp"), None)
    return jax.shard_map(
        local,
        mesh=mesh,
        in_specs=(shard, shard, shard, P(), P()),
        out_specs=(shard, shard),
        check_vma=False,
    )
```

time: 72.9 us -> 68.7 us (0.942)
  Pallas kernels: 70.8 us -> 66.6 us
    pallas_call x1, Pallas kernels: 69.6 us -> 65.3 us  [local(): pl.pallas_call(functools.partial(kernel, groups, total), out_shape=(pltpu...]
where the time goes in v2:
time: 68.7 us; the launch traced here: 68.5 us
  Pallas kernels  66.6 us (97%)
  between operations  1.93 us (3%)
    pallas_call x1, Pallas kernels, local(): pl.pallas_call(functools.partial(kernel, groups, total), out_shape=(pltpu...  65.3 us

profile of v2, /device:TPU:0, one launch (start us, length us, event | category | flops | bytes accessed | tf_op | source)
XLA Modules:
  0.0 68.5 jit_solution(15164078736327780272)
XLA Ops:
  1.9 65.3 %shard_map.68 = (bf16[384,1152]{1,0:T(8,128)(2,1)S(1)}, bf16[384,1152]{1,0:T(8,128)(2,1)S(1)}) custom-call(bf16[384,1152]{1,0:T(8,128)(2,1)} %image_hbm.1, bf16[384,1152]{1,0:T(8,128)(2,1)} %text_hbm.1, s32[1,384]{1,0:T(1,128)} %position_hbm.1, f32[1]{0:T(128)S(6)} %copy.7.exponent_ref, f32[1]{0:T(128)S(6)} %copy.8.offset_ref), custom_call_target="tpu_custom_call" | custom-call | tf_op jit(solution)/shard_map/pallas_call | solution.py:295
  67.3 1.2 %shard_map.69 = (bf16[384,1152]{1,0:T(8,128)(2,1)}, bf16[384,1152]{1,0:T(8,128)(2,1)}) custom-call(bf16[384,1152]{1,0:T(8,128)(2,1)S(1)} %get-tuple-element.4.image_grad, bf16[384,1152]{1,0:T(8,128)(2,1)S(1)} %get-tuple-element.5.text_grad), custom_call_target="tpu_custom_call" | custom-call | tf_op jit(solution)/shard_map/pallas_call | solution.py:328

commit v3 on v2

--- a/solution.py
+++ b/solution.py
@@ -8,12 +8,140 @@
 from jax.sharding import PartitionSpec as P
 
 CHUNKS = 3
-NORM_ROWS = 32
+NORM_ROWS = 64
 MESH = pl.DeviceIdType.MESH
 
 F0, F1, F2, N0, N1 = range(5)
 OWN_F0, OWN_F1, OWN_N0, OWN_N1, PAIR_F1, PAIR_F2, PAIR_N0, PAIR_N1 = range(8)
-FAR, HOP, NEAR, SUM_F2, SUM_F1, SUM_N1, IMAGE, SUM_IMAGE = range(8)
+IN_F1, IN_F2, IN_N1, IN_IMAGE, BACK_F2, BACK_F1, HOME, HOME_SPLIT, HOME_N, HOME_IMAGE = range(10)
+(FAR, SPLIT, HOP, TURN, NEAR, IMAGE, SUM_F2, SUM_F1, SUM_N1, SUM_IMAGE) = range(10)
+
+(
+    UNIT_F,
+    UNIT_N,
+    UNIT_IMAGE,
+    ENTER,
+    READY,
+    PUT_FAR,
+    PUT_FAR_LOW,
+    PUT_NEAR,
+    PUT_NEAR_LOW,
+    PUT_SPLIT,
+    PUT_SPLIT_LOW,
+    PUT_IMAGE,
+    HOP_FIRST,
+    HOP_LATER,
+    TURN_BACK,
+    TILE_F0,
+    TILE_N0,
+    TILE_F1,
+    TILE_N1,
+    CROSS_N0,
+    CROSS_N1,
+    CROSS_F1,
+    CROSS_F2,
+    PASS_F2,
+    PASS_F1_FIRST,
+    PASS_F1_LATER,
+    GATHER_PAIR,
+    GATHER_OWN,
+    END_IMAGE,
+    END_N,
+    END_F,
+) = range(31)
+
+ORDER = (
+    (UNIT_F, 0),
+    (UNIT_F, 1),
+    (ENTER, 0),
+    (PUT_SPLIT, 0),
+    (PUT_FAR, 0),
+    (PUT_FAR, 1),
+    (UNIT_IMAGE, 0),
+    (UNIT_N, 0),
+    (UNIT_N, 1),
+    (UNIT_N, 2),
+    (UNIT_IMAGE, 1),
+    (PUT_IMAGE, 0),
+    (UNIT_F, 2),
+    (PUT_NEAR, 0),
+    (PUT_FAR, 2),
+    (READY, 0),
+    (UNIT_IMAGE, 2),
+    (HOP_LATER, 0),
+    (PUT_SPLIT_LOW, 0),
+    (PUT_NEAR_LOW, 0),
+    (PUT_NEAR, 1),
+    (PUT_NEAR_LOW, 1),
+    (HOP_FIRST, 0),
+    (PUT_SPLIT, 1),
+    (PUT_IMAGE, 1),
+    (HOP_FIRST, 1),
+    (PUT_NEAR_LOW, 2),
+    (TURN_BACK, 0),
+    (PUT_IMAGE, 2),
+    (HOP_FIRST, 2),
+    (PUT_FAR_LOW, 0),
+    (PUT_FAR_LOW, 1),
+    (PUT_FAR_LOW, 2),
+    (PUT_SPLIT_LOW, 1),
+    (PUT_SPLIT, 2),
+    (TILE_F0, 0),
+    (TURN_BACK, 1),
+    (TURN_BACK, 2),
+    (PUT_NEAR, 2),
+    (HOP_LATER, 1),
+    (TILE_F1, 0),
+    (TILE_N0, 0),
+    (PUT_SPLIT_LOW, 2),
+    (CROSS_F1, 0),
+    (CROSS_F2, 0),
+    (TILE_F1, 1),
+    (TILE_F1, 2),
+    (HOP_LATER, 2),
+    (CROSS_F1, 1),
+    (CROSS_F1, 2),
+    (TILE_N1, 0),
+    (CROSS_N0, 0),
+    (TILE_N1, 1),
+    (CROSS_N1, 0),
+    (PASS_F2, 0),
+    (CROSS_F2, 1),
+    (PASS_F2, 1),
+    (PASS_F1_LATER, 0),
+    (CROSS_F2, 2),
+    (PASS_F2, 2),
+    (CROSS_N1, 1),
+    (TILE_N1, 2),
+    (PASS_F1_FIRST, 0),
+    (CROSS_N1, 2),
+    (GATHER_PAIR, 0),
+    (GATHER_OWN, 0),
+    (GATHER_PAIR, 1),
+    (GATHER_PAIR, 2),
+    (PASS_F1_LATER, 1),
+    (GATHER_OWN, 1),
+    (END_F, 0),
+    (END_N, 0),
+    (PASS_F1_FIRST, 1),
+    (PASS_F1_LATER, 2),
+    (END_IMAGE, 0),
+    (GATHER_OWN, 2),
+    (PASS_F1_FIRST, 2),
+    (END_IMAGE, 1),
+    (END_N, 1),
+    (END_F, 1),
+    (END_IMAGE, 2),
+    (END_N, 2),
+    (END_F, 2),
+)
+
+SLOT_OF = {CROSS_N0: N0, CROSS_N1: N1, CROSS_F1: F1, CROSS_F2: F2}
+CROSSES = tuple(SLOT_OF[name] for name, _ in ORDER if name in SLOT_OF)
+
+
+def starts(one, other):
+    return ORDER.index(one) < ORDER.index(other)
 
 
 def kernel(
@@ -44,6 +172,7 @@
     load_sem,
     send_sem,
     recv_sem,
+    ready_sem,
 ):
     rows, width = image_hbm.shape
     half = rows // 2
@@ -57,12 +186,60 @@
         return (index // groups, lax.rem(index, groups))
 
     pair = place(me + 1 - 2 * parity)
-    far = place(me + reach)
-    near = place(me - reach)
-
+    far, far_two = place(me + reach), place(me + 2 * reach)
+    near, near_two = place(me - reach), place(me - 2 * reach)
+
+    line = groups // 2
+    z = lax.axis_index("grp") // 2
+    since = parity * z + (1 - parity) * (line - 1 - z)
+    until = line - 1 - since
+
+    even, odd = parity == 0, parity == 1
+    first = (since == 1) & (until > 0)
+    later = (since > 1) & (until > 0)
+
+    below, below_two = place(me - 2), place(me - 4)
+    above, above_two = place(me + 2), place(me + 4)
     barrier = pltpu.get_barrier_semaphore()
-    for device in (pair, far, near):
-        pl.semaphore_signal(barrier, inc=1, device_id=device, device_id_type=MESH)
+
+    def greet(sem, device):
+        pl.semaphore_signal(sem, inc=1, device_id=device, device_id_type=MESH)
+
+    greet(barrier, pair)
+    greet(barrier, below)
+
+    @pl.when(z < line - 1)
+    def _():
+        greet(barrier, above)
+
+    @pl.when(z <= 1)
+    def _():
+        greet(barrier, below_two)
+
+    def enter():
+        for start in (False, True):
+            for end in (False, True):
+
+                @pl.when(((z == 0) == start) & ((z >= line - 2) == end))
+                def _():
+                    pl.semaphore_wait(barrier, 3 - start + end)
+
+        @pl.when(z >= line - 2)
+        def _():
+            greet(ready_sem, above_two)
+
+        @pl.when(z == line - 1)
+        def _():
+            greet(ready_sem, above)
+
+    def ready():
+        @pl.when(z == 0)
+        def _():
+            pl.semaphore_wait(ready_sem, 2)
+
+        @pl.when(z == 1)
+        def _():
+            pl.semaphore_wait(ready_sem, 1)
 
     start_f = pl.multiple_of(half - parity * half, half)
     start_n = pl.multiple_of(parity * half, half)
@@ -81,71 +258,64 @@
         copy.start()
 
     def piece(c):
-        return pl.ds(c * chunk, chunk)
+        return pl.ds(0, half) if c is None else pl.ds(c * chunk, chunk)
 
     def stripe(c):
         return pl.ds(c * band, band)
 
-    routes = {
-        FAR: (captions.at[F0], captions.at[F1], far, piece),
-        HOP: (captions.at[F1], captions.at[F2], far, piece),
-        NEAR: (captions.at[N0], captions.at[N1], near, piece),
-        SUM_F2: (staged.at[0], returned.at[0], near, piece),
-        SUM_F1: (staged.at[1], returned.at[1], near, piece),
-        SUM_N1: (staged.at[2], returned.at[2], far, piece),
-        IMAGE: (image_unit, pair_unit, pair, stripe),
-        SUM_IMAGE: (image_staged, image_returned, pair, stripe),
-    }
-
-    def message(name, c):
-        source, target, device, part = routes[name]
+    def message(name, arrival, source, target, device, part, c):
         return pltpu.make_async_remote_copy(
             src_ref=source.at[part(c)],
             dst_ref=target.at[part(c)],
             send_sem=send_sem.at[name, c],
-            recv_sem=recv_sem.at[name, c],
+            recv_sem=recv_sem.at[arrival, c],
             device_id=device,
             device_id_type=MESH,
         )
 
-    def send(name, c):
-        message(name, c).start()
-
-    def receive(name, c):
-        message(name, c).wait_recv()
-
-    def normalize(source, inverse, target, source_start):
+    landing = {
+        IN_F1: (captions.at[F1], piece),
+        IN_F2: (captions.at[F2], piece),
+        IN_N1: (captions.at[N1], piece),
+        IN_IMAGE: (pair_unit, stripe),
+        BACK_F2: (returned.at[0], piece),
+        BACK_F1: (returned.at[1], piece),
+        HOME: (returned.at[2], piece),
+        HOME_SPLIT: (returned.at[3], piece),
+        HOME_N: (returned.at[4], piece),
+        HOME_IMAGE: (image_returned, stripe),
+    }
+
+    def send(name, arrival, source, device, c):
+        target, part = landing[arrival]
+        message(name, arrival, source, target, device, part, c).start()
+
+    def receive(arrival, c):
+        target, part = landing[arrival]
+        message(0, arrival, target, target, pair, part, c).wait_recv()
+
+    def sent(name, source, part):
+        for c in range(CHUNKS):
+            message(name, 0, source, source, pair, part, c).wait_send()
+
+    def normalize(source, inverse, target, source_start, at, count):
         def body(i, carry):
-            at = pl.multiple_of(i * NORM_ROWS, NORM_ROWS)
-            here = pl.ds(pl.multiple_of(source_start + at, NORM_ROWS), NORM_ROWS)
+            local = pl.multiple_of(at + i * NORM_ROWS, NORM_ROWS)
+            here = pl.ds(pl.multiple_of(source_start + local, NORM_ROWS), NORM_ROWS)
             values = source[here, :].astype(jnp.float32)
             scale = lax.rsqrt(jnp.sum(values * values, axis=1, keepdims=True) + 1e-06)
             inverse[here, :] = scale
-            target[pl.ds(at, NORM_ROWS), :] = (values * scale).astype(jnp.bfloat16)
+            target[pl.ds(local, NORM_ROWS), :] = (values * scale).astype(jnp.bfloat16)
             return carry
 
-        lax.fori_loop(0, target.shape[0] // NORM_ROWS, body, 0)
-
-    loads[0].wait()
-    normalize(text_ref, text_inverse, captions.at[F0], start_f)
-    pl.semaphore_wait(barrier, 3)
-    for c in range(CHUNKS):
-        send(FAR, c)
-    loads[1].wait()
-    normalize(text_ref, text_inverse, captions.at[N0], start_n)
-    for c in range(CHUNKS):
-        send(NEAR, c)
-    for copy in loads[2:]:
-        copy.wait()
-    normalize(image_ref, image_inverse, image_unit, 0)
-    for c in range(CHUNKS):
-        send(IMAGE, c)
+        lax.fori_loop(0, count // NORM_ROWS, body, 0)
 
     scale = jnp.exp(jnp.full((1, rows), exponent_ref[0], jnp.float32))
     offset = offset_ref[0]
 
     def tile(slot, images, table, c, first_row=None):
-        text = captions[slot, piece(c), :]
+        here = piece(c)
+        text = captions[slot, here, :]
         logit = (
             lax.dot_general(
                 text,
@@ -159,11 +329,11 @@
         if first_row is None:
             coef = scale * jax.nn.sigmoid(logit)
         else:
-            row = lax.broadcasted_iota(jnp.int32, logit.shape, 0) + first_row + c * chunk
+            row = lax.broadcasted_iota(jnp.int32, logit.shape, 0) + first_row + (c or 0) * chunk
             polarity = jnp.where(row == position_ref[0:1, :], 1.0, -1.0)
             coef = scale * (-polarity * jax.nn.sigmoid(-polarity * logit))
         coef = coef.astype(jnp.bfloat16)
-        coefs[table, piece(c), :] = coef
+        coefs[table, here, :] = coef
         return jnp.dot(coef, images[...], preferred_element_type=jnp.float32)
 
     def keep(part, c, value):
@@ -213,59 +383,245 @@
 
         lax.fori_loop(0, chunk // NORM_ROWS, body, 0)
 
-    for c in range(CHUNKS):
-        keep(F0, c, tile(F0, image_unit, OWN_F0, c, start_f))
-    for c in range(CHUNKS):
-        receive(FAR, c)
-        send(HOP, c)
-        keep(N0, c, tile(N0, image_unit, OWN_N0, c, start_n))
-    for c in range(CHUNKS):
+    def unit_f(c):
+        if c == 0:
+            loads[0].wait()
+        normalize(text_ref, text_inverse, captions.at[F0], start_f, c * chunk, chunk)
+
+    def unit_n(c):
+        if c == 0:
+            loads[1].wait()
+        normalize(text_ref, text_inverse, captions.at[N0], start_n, c * chunk, chunk)
+
+    def unit_image(c):
+        if c == 0:
+            loads[2].wait()
+            loads[3].wait()
+        normalize(image_ref, image_inverse, image_unit, 0, c * band, band)
+
+    def put_far(low):
+        def run(c):
+            @pl.when((until == 0) & (even if low else odd))
+            def _():
+                send(FAR, IN_F2, captions.at[F0], far_two, c)
+
+            if not low:
+                @pl.when(until > 0)
+                def _():
+                    send(FAR, IN_F1, captions.at[F0], far, c)
+
+        return run
+
+    def put_split(low):
+        def run(c):
+            @pl.when((until == 1) & (even if low else odd))
+            def _():
+                send(SPLIT, IN_F2, captions.at[F0], far_two, c)
+
+        return run
+
+    def put_near(low):
+        wraps = (since == 0) & odd
+
+        def run(c):
+            @pl.when(wraps if low else jnp.logical_not(wraps))
+            def _():
+                send(NEAR, IN_N1, captions.at[N0], near, c)
+
+        return run
+
+    def put_image(c):
+        send(IMAGE, IN_IMAGE, image_unit, pair, c)
+
+    def hop(condition, op):
+        def run(c):
+            @pl.when(condition)
+            def _():
+                if starts((op, c), (TILE_F1, c)):
+                    receive(IN_F1, c)
+                send(HOP, IN_F2, captions.at[F1], far, c)
+
+        return run
+
+    def turn_back(c):
+        @pl.when(since == 1)
+        def _():
+            if starts((TURN_BACK, c), (CROSS_F2, c)):
+                receive(IN_F2, c)
+            send(TURN, IN_F1, captions.at[F2], near, c)
+
+    def tile_f0(c):
+        keep(F0, None, tile(F0, image_unit, OWN_F0, None, start_f))
+
+    def tile_n0(c):
+        keep(N0, None, tile(N0, image_unit, OWN_N0, None, start_n))
+
+    def tile_f1(c):
+        waits = (since == 0) | (until == 0)
+        if not starts((HOP_FIRST, c), (TILE_F1, c)):
+            waits = waits | first
+        if not starts((HOP_LATER, c), (TILE_F1, c)):
+            waits = waits | later
+
+        @pl.when(waits)
+        def _():
+            receive(IN_F1, c)
+
         keep(F1, c, tile(F1, image_unit, OWN_F1, c))
-    for c in range(CHUNKS):
-        receive(NEAR, c)
+
+    def tile_n1(c):
+        receive(IN_N1, c)
         keep(N1, c, tile(N1, image_unit, OWN_N1, c))
 
-    for c in range(CHUNKS):
-        receive(IMAGE, c)
-    for c in range(CHUNKS):
-        give(2, c, partial[N1, piece(c), :] + tile(N1, pair_unit, PAIR_N1, c))
-        send(SUM_N1, c)
-    for c in range(CHUNKS):
-        add(F1, c, tile(F1, pair_unit, PAIR_F1, c))
-    for c in range(CHUNKS):
-        receive(HOP, c)
-        give(0, c, tile(F2, pair_unit, PAIR_F2, c))
-        send(SUM_F2, c)
-    for c in range(CHUNKS):
-        add(N0, c, tile(N0, pair_unit, PAIR_N0, c))
+    def cross(slot, table, c, whole=False):
+        if (CROSSES[0], 0) == (slot, c):
+            for i in range(CHUNKS):
+                receive(IN_IMAGE, i)
+        return tile(slot, pair_unit, table, None if whole else c)
+
+    def cross_n0(c):
+        add(N0, None, cross(N0, PAIR_N0, c, True))
+
+    def cross_n1(c):
+        give(2, c, partial[N1, piece(c), :] + cross(N1, PAIR_N1, c))
+        send(SUM_N1, HOME_N, staged.at[2], far, c)
+
+    def cross_f1(c):
+        add(F1, c, cross(F1, PAIR_F1, c))
+
+        @pl.when(since == 0)
+        def _():
+            give(1, c, partial[F1, piece(c), :])
+            send(SUM_F1, BACK_F1, staged.at[1], far, c)
+
+        @pl.when(until == 0)
+        def _():
+            give(1, c, partial[F1, piece(c), :])
+            send(SUM_F1, HOME, staged.at[1], near, c)
+
+    def cross_f2(c):
+        waits = since != 1
+        if not starts((TURN_BACK, c), (CROSS_F2, c)):
+            waits = since >= 0
+
+        @pl.when(waits)
+        def _():
+            receive(IN_F2, c)
+
+        keep(F2, c, cross(F2, PAIR_F2, c))
+
+        @pl.when(since == 0)
+        def _():
+            give(0, c, partial[F2, piece(c), :])
+            send(SUM_F2, HOME_SPLIT, staged.at[0], near_two, c)
+
+        @pl.when(since > 1)
+        def _():
+            give(0, c, partial[F2, piece(c), :])
+            send(SUM_F2, BACK_F2, staged.at[0], near, c)
+
+    def pass_f2(c):
+        @pl.when(since == 1)
+        def _():
+            receive(BACK_F1, c)
+            arrived = returned[1, piece(c), :].astype(jnp.float32)
+            give(0, c, arrived + partial[F2, piece(c), :])
+            send(SUM_F2, HOME, staged.at[0], near_two, c)
+
+    def pass_f1(condition):
+        def run(c):
+            @pl.when(condition)
+            def _():
+                receive(BACK_F2, c)
+                arrived = returned[0, piece(c), :].astype(jnp.float32)
+                give(1, c, arrived + partial[F1, piece(c), :])
+                send(SUM_F1, HOME, staged.at[1], near, c)
+
+        return run
 
     pair_terms = ((PAIR_F1, F1), (PAIR_F2, F2), (PAIR_N0, N0), (PAIR_N1, N1))
-    for c in range(CHUNKS):
+    own_terms = ((OWN_F0, F0), (OWN_F1, F1), (OWN_N0, N0), (OWN_N1, N1))
+
+    def gather_pair(c):
         image_staged[stripe(c), :] = gather(c, pair_terms).astype(jnp.bfloat16)
-        send(SUM_IMAGE, c)
-
-    for c in range(CHUNKS):
-        receive(SUM_F2, c)
-        arrived = returned[0, piece(c), :].astype(jnp.float32)
-        give(1, c, arrived + partial[F1, piece(c), :])
-        send(SUM_F1, c)
-
-    own_terms = ((OWN_F0, F0), (OWN_F1, F1), (OWN_N0, N0), (OWN_N1, N1))
-    for c in range(CHUNKS):
+        send(SUM_IMAGE, HOME_IMAGE, image_staged, pair, c)
+
+    def gather_own(c):
         direction[stripe(c), :] = gather(c, own_terms)
-    for c in range(CHUNKS):
-        receive(SUM_IMAGE, c)
+
+    def end_image(c):
+        receive(HOME_IMAGE, c)
         finish_images(c)
-    for c in range(CHUNKS):
-        receive(SUM_N1, c)
-        finish_text(c, start_n, N0, 2)
-    for c in range(CHUNKS):
-        receive(SUM_F1, c)
-        finish_text(c, start_f, F0, 1)
-
-    for name in routes:
-        for c in range(CHUNKS):
-            message(name, c).wait_send()
+
+    def end_n(c):
+        receive(HOME_N, c)
+        finish_text(c, start_n, N0, 4)
+
+    def end_f(c):
+        receive(HOME, c)
+
+        @pl.when(until == 1)
+        def _():
+            receive(HOME_SPLIT, c)
+            add(F0, c, returned[3, piece(c), :].astype(jnp.float32))
+
+        finish_text(c, start_f, F0, 2)
+
+    steps = {
+        UNIT_F: unit_f,
+        UNIT_N: unit_n,
+        UNIT_IMAGE: unit_image,
+        ENTER: lambda c: enter(),
+        READY: lambda c: ready(),
+        PUT_FAR: put_far(False),
+        PUT_FAR_LOW: put_far(True),
+        PUT_NEAR: put_near(False),
+        PUT_NEAR_LOW: put_near(True),
+        PUT_SPLIT: put_split(False),
+        PUT_SPLIT_LOW: put_split(True),
+        PUT_IMAGE: put_image,
+        HOP_FIRST: hop(first, HOP_FIRST),
+        HOP_LATER: hop(later, HOP_LATER),
+        TURN_BACK: turn_back,
+        TILE_F0: tile_f0,
+        TILE_N0: tile_n0,
+        TILE_F1: tile_f1,
+        TILE_N1: tile_n1,
+        CROSS_N0: cross_n0,
+        CROSS_N1: cross_n1,
+        CROSS_F1: cross_f1,
+        CROSS_F2: cross_f2,
+        PASS_F2: pass_f2,
+        PASS_F1_FIRST: pass_f1(first),
+        PASS_F1_LATER: pass_f1(later),
+        GATHER_PAIR: gather_pair,
+        GATHER_OWN: gather_own,
+        END_IMAGE: end_image,
+        END_N: end_n,
+        END_F: end_f,
+    }
+    for name, c in ORDER:
+        steps[name](c)
+
+    sent(FAR, captions.at[F0], piece)
+    sent(NEAR, captions.at[N0], piece)
+    sent(IMAGE, image_unit, stripe)
+    sent(SUM_F2, staged.at[0], piece)
+    sent(SUM_F1, staged.at[1], piece)
+    sent(SUM_N1, staged.at[2], piece)
+    sent(SUM_IMAGE, image_staged, stripe)
+
+    @pl.when(until == 1)
+    def _():
+        sent(SPLIT, captions.at[F0], piece)
+
+    @pl.when((since > 0) & (until > 0))
+    def _():
+        sent(HOP, captions.at[F1], piece)
+
+    @pl.when(since == 1)
+    def _():
+        sent(TURN, captions.at[F2], piece)
 
 
 def store(image_grad, text_grad, image_out, text_out, sem):
@@ -310,15 +666,16 @@
                 pltpu.VMEM((8, half, rows), jnp.bfloat16),
                 pltpu.VMEM((5, half, width), jnp.float32),
                 pltpu.VMEM((3, half, width), jnp.bfloat16),
-                pltpu.VMEM((3, half, width), jnp.bfloat16),
+                pltpu.VMEM((5, half, width), jnp.bfloat16),
                 pltpu.VMEM((rows, width), jnp.bfloat16),
                 pltpu.VMEM((rows, width), jnp.bfloat16),
                 pltpu.VMEM((rows, width), jnp.float32),
                 pltpu.VMEM((rows, 1), jnp.float32),
                 pltpu.VMEM((rows, 1), jnp.float32),
                 pltpu.SemaphoreType.DMA((4,)),
-                pltpu.SemaphoreType.DMA((8, CHUNKS)),
-                pltpu.SemaphoreType.DMA((8, CHUNKS)),
+                pltpu.SemaphoreType.DMA((10, CHUNKS)),
+                pltpu.SemaphoreType.DMA((10, CHUNKS)),
+                pltpu.SemaphoreType.REGULAR,
             ],
             compiler_params=pltpu.CompilerParams(
                 collective_id=0, has_side_effects=True, vmem_limit_bytes=32 * 1024 * 1024

time: 68.7 us -> 65.5 us (0.953)
  the two profiles are of different devices: /device:TPU:0 before, /device:TPU:16 now
where the time goes in v3:
time: 65.5 us; the launch traced here: 65.4 us
  Pallas kernels  63.4 us (97%)
  between operations  1.93 us (3%)
    pallas_call x1, Pallas kernels, local(): pl.pallas_call(functools.partial(kernel, groups, total), out_shape=(pltpu...  62.2 us

profile of v3, /device:TPU:16, one launch (start us, length us, event | category | flops | bytes accessed | tf_op | source)
XLA Modules:
  0.0 65.4 jit_solution(17854081157072333782)
XLA Ops:
  1.9 62.2 %shard_map.68 = (bf16[384,1152]{1,0:T(8,128)(2,1)S(1)}, bf16[384,1152]{1,0:T(8,128)(2,1)S(1)}) custom-call(bf16[384,1152]{1,0:T(8,128)(2,1)} %image_hbm.1, bf16[384,1152]{1,0:T(8,128)(2,1)} %text_hbm.1, s32[1,384]{1,0:T(1,128)} %position_hbm.1, f32[1]{0:T(128)S(6)} %copy.7.exponent_ref, f32[1]{0:T(128)S(6)} %copy.8.offset_ref), custom_call_target="tpu_custom_call" | custom-call | tf_op jit(solution)/shard_map/pallas_call | solution.py:651
  64.1 1.2 %shard_map.69 = (bf16[384,1152]{1,0:T(8,128)(2,1)}, bf16[384,1152]{1,0:T(8,128)(2,1)}) custom-call(bf16[384,1152]{1,0:T(8,128)(2,1)S(1)} %get-tuple-element.4.image_grad, bf16[384,1152]{1,0:T(8,128)(2,1)S(1)} %get-tuple-element.5.text_grad), custom_call_target="tpu_custom_call" | custom-call | tf_op jit(solution)/shard_map/pallas_call | solution.py:685

commit v4 on v3

--- a/solution.py
+++ b/solution.py
@@ -53,18 +53,18 @@
 ORDER = (
     (UNIT_F, 0),
     (UNIT_F, 1),
+    (UNIT_N, 0),
     (ENTER, 0),
     (PUT_SPLIT, 0),
     (PUT_FAR, 0),
     (PUT_FAR, 1),
+    (PUT_NEAR, 0),
     (UNIT_IMAGE, 0),
-    (UNIT_N, 0),
     (UNIT_N, 1),
     (UNIT_N, 2),
     (UNIT_IMAGE, 1),
     (PUT_IMAGE, 0),
     (UNIT_F, 2),
-    (PUT_NEAR, 0),
     (PUT_FAR, 2),
     (READY, 0),
     (UNIT_IMAGE, 2),
@@ -125,13 +125,13 @@
     (END_N, 0),
     (PASS_F1_FIRST, 1),
     (PASS_F1_LATER, 2),
+    (GATHER_OWN, 2),
     (END_IMAGE, 0),
-    (GATHER_OWN, 2),
     (PASS_F1_FIRST, 2),
     (END_IMAGE, 1),
+    (END_IMAGE, 2),
     (END_N, 1),
     (END_F, 1),
-    (END_IMAGE, 2),
     (END_N, 2),
     (END_F, 2),
 )

time: 65.5 us -> 65.5 us (level)
  no operation moved by 1% of the time
where the time goes in v4:
time: 65.5 us; the launch traced here: 65.4 us
  Pallas kernels  63.4 us (97%)
  between operations  1.93 us (3%)
    pallas_call x1, Pallas kernels, local(): pl.pallas_call(functools.partial(kernel, groups, total), out_shape=(pltpu...  62.2 us

profile of v4, /device:TPU:16, one launch (start us, length us, event | category | flops | bytes accessed | tf_op | source)
XLA Modules:
  0.0 65.4 jit_solution(8035541109179536785)
XLA Ops:
  1.9 62.2 %shard_map.68 = (bf16[384,1152]{1,0:T(8,128)(2,1)S(1)}, bf16[384,1152]{1,0:T(8,128)(2,1)S(1)}) custom-call(bf16[384,1152]{1,0:T(8,128)(2,1)} %image_hbm.1, bf16[384,1152]{1,0:T(8,128)(2,1)} %text_hbm.1, s32[1,384]{1,0:T(1,128)} %position_hbm.1, f32[1]{0:T(128)S(6)} %copy.7.exponent_ref, f32[1]{0:T(128)S(6)} %copy.8.offset_ref), custom_call_target="tpu_custom_call" | custom-call | tf_op jit(solution)/shard_map/pallas_call | solution.py:651
  64.1 1.2 %shard_map.69 = (bf16[384,1152]{1,0:T(8,128)(2,1)}, bf16[384,1152]{1,0:T(8,128)(2,1)}) custom-call(bf16[384,1152]{1,0:T(8,128)(2,1)S(1)} %get-tuple-element.4.image_grad, bf16[384,1152]{1,0:T(8,128)(2,1)S(1)} %get-tuple-element.5.text_grad), custom_call_target="tpu_custom_call" | custom-call | tf_op jit(solution)/shard_map/pallas_call | solution.py:685

commit v5 on v3

--- a/solution.py
+++ b/solution.py
@@ -625,10 +625,15 @@
 
 
 def store(image_grad, text_grad, image_out, text_out, sem):
-    copies = (
-        pltpu.make_async_copy(image_grad, image_out, sem.at[0]),
-        pltpu.make_async_copy(text_grad, text_out, sem.at[1]),
-    )
+    parts = sem.shape[1]
+    share = image_grad.shape[0] // parts
+    copies = [
+        pltpu.make_async_copy(
+            source.at[pl.ds(c * share, share)], target.at[pl.ds(c * share, share)], sem.at[n, c]
+        )
+        for c in range(parts)
+        for n, (source, target) in enumerate(((image_grad, image_out), (text_grad, text_out)))
+    ]
     for copy in copies:
         copy.start()
     for copy in copies:
@@ -687,7 +692,7 @@
             out_shape=(jax.ShapeDtypeStruct((rows, width), jnp.bfloat16),) * 2,
             in_specs=[vmem, vmem],
             out_specs=(hbm, hbm),
-            scratch_shapes=[pltpu.SemaphoreType.DMA((2,))],
+            scratch_shapes=[pltpu.SemaphoreType.DMA((2, 4))],
         )(*grads)
 
     shard = P(("blk", "grp"), None)

time: 65.5 us -> 65.6 us (level)
  no operation moved by 1% of the time
where the time goes in v5:
time: 65.6 us; the launch traced here: 65.4 us
  Pallas kernels  63.5 us (97%)
  between operations  1.93 us (3%)
    pallas_call x1, Pallas kernels, local(): pl.pallas_call(functools.partial(kernel, groups, total), out_shape=(pltpu...  62.2 us

profile of v5, /device:TPU:16, one launch (start us, length us, event | category | flops | bytes accessed | tf_op | source)
XLA Modules:
  0.0 65.4 jit_solution(4857204126830641713)
XLA Ops:
  1.9 62.2 %shard_map.68 = (bf16[384,1152]{1,0:T(8,128)(2,1)S(1)}, bf16[384,1152]{1,0:T(8,128)(2,1)S(1)}) custom-call(bf16[384,1152]{1,0:T(8,128)(2,1)} %image_hbm.1, bf16[384,1152]{1,0:T(8,128)(2,1)} %text_hbm.1, s32[1,384]{1,0:T(1,128)} %position_hbm.1, f32[1]{0:T(128)S(6)} %copy.7.exponent_ref, f32[1]{0:T(128)S(6)} %copy.8.offset_ref), custom_call_target="tpu_custom_call" | custom-call | tf_op jit(solution)/shard_map/pallas_call | solution.py:656
  64.1 1.3 %shard_map.69 = (bf16[384,1152]{1,0:T(8,128)(2,1)}, bf16[384,1152]{1,0:T(8,128)(2,1)}) custom-call(bf16[384,1152]{1,0:T(8,128)(2,1)S(1)} %get-tuple-element.4.image_grad, bf16[384,1152]{1,0:T(8,128)(2,1)S(1)} %get-tuple-element.5.text_grad), custom_call_target="tpu_custom_call" | custom-call | tf_op jit(solution)/shard_map/pallas_call | solution.py:690
